TPU v7x, 512 devices: a whole 4x8x8 slice. The times are simulated.
512 devices in a mesh: pipe: 8 (over z), ctx: 32 (over x, y_hi, core), tp: 2 (over y_lo).
Axes of the slice: x: 4, y: 8 (y_hi: 4, y_lo: 2; y = y_hi * 2 + y_lo), z: 8, core: 2. Of those that a mesh axis runs over, the one named last changes fastest.
Arguments:
- queries: bfloat16 [8, 2048, 128, 128], P('pipe', 'ctx', 'tp'), may hold values from -10 to 10
- span_keys: bfloat16 [8, 2048, 8, 128], P('pipe', 'ctx', 'tp'), may hold values from -6 to 6
- span_values: bfloat16 [8, 2048, 8, 128], P('pipe', 'ctx', 'tp'), may hold values from -12 to 12
- cache_keys: bfloat16 [8, 1024, 8, 128], P('pipe', 'ctx', 'tp'), may hold values from -6 to 6
- cache_values: bfloat16 [8, 1024, 8, 128], P('pipe', 'ctx', 'tp'), may hold values from -6 to 6
- scale_exps: int32 [8, 64, 8, 2], P('pipe', 'ctx', 'tp'), may hold values from -3 to 1
- block_order: int32 [8, 64], P('pipe'), may hold values from 0 to 63, each once within a row
Outputs:
- handed: bfloat16 [8, 2048, 128, 128], P('pipe', 'ctx', 'tp')
All inputs are finite; a program needn't handle non-finite values.
Results may differ from a plain program's by a relative error of at most 0.006.
Values may be sent and summed in bfloat16 or wider, within the bound.
No kernel may reach another device: no remote copies, remote signals or barrier semaphores. Data moves between devices by JAX's collectives and lax.ppermute only.
A program may use at most 128 MiB of HBM per device.

v0:
```python
import jax
import jax.numpy as jnp
from jax import lax
from jax.sharding import PartitionSpec as P

CBLK = 16


def shifted(value, axis, steps):
    count = lax.axis_size(axis)
    pairs = [(source, (source + steps) % count) for source in range(count)]
    return lax.ppermute(value, axis, pairs)


def hadamard(order):
    rows = jnp.arange(order, dtype=jnp.int32)[:, None]
    cols = jnp.arange(order, dtype=jnp.int32)[None, :]
    common = jnp.zeros((order, order), jnp.int32)
    for bit in range(order.bit_length() - 1):
        common = common + (jnp.right_shift(rows, bit) & 1) * (jnp.right_shift(cols, bit) & 1)
    signs = 1.0 - 2.0 * (common % 2).astype(jnp.float32)
    return signs * (1.0 / order**0.5)


def table_lookup(table, slots):
    match = jnp.arange(table.shape[0], dtype=jnp.int32)[None, :] == slots[:, None]
    return jnp.sum(jnp.where(match, table[None, :], 0), axis=1)


def attend(carry, block, grouped, pos_query, order, half, cache_len, rows_dev):
    best, total, accum = carry
    keys = block[:, :, 0, :]
    vals = block[:, :, 1, :]
    count = block.shape[0]
    global_row = jnp.arange(count, dtype=jnp.int32)
    owner = global_row // rows_dev
    local = global_row % rows_dev
    offset = jnp.maximum(local - cache_len, 0)
    pos_key = table_lookup(order, 2 * owner + offset // half) * half + offset % half
    visible = (local < cache_len)[None, :] | (pos_key[None, :] <= pos_query[:, None])
    inv = 1.0 / grouped.shape[-1] ** 0.5
    score = jnp.einsum("tgqd,kgd->gqtk", grouped, keys, preferred_element_type=jnp.float32) * inv
    score = jnp.where(visible[None, None], score, -jnp.inf)
    best_new = jnp.max(score, axis=-1)
    safe = jnp.where(best_new == -jnp.inf, 0.0, best_new)
    expo = jnp.exp(score - safe[..., None])
    rescale = jnp.exp(best - safe)
    total = total * rescale + jnp.sum(expo, axis=-1)
    accum = accum * rescale[..., None] + jnp.einsum(
        "gqtk,kgd->gqtd", expo.astype(jnp.bfloat16), vals, preferred_element_type=jnp.float32
    )
    return (best_new, total, accum)


def on_device(queries, span_keys, span_values, cache_keys, cache_values, scale_exps, block_order):
    mine = lax.axis_index("ctx")
    tok_local = queries.shape[1]
    head_local = queries.shape[2]
    kv_local = span_keys.shape[2]
    width = queries.shape[3]
    cache_len = cache_keys.shape[1]
    half = tok_local // 2
    rows_dev = cache_len + tok_local
    grouped = queries[0].reshape(tok_local, kv_local, head_local // kv_local, width)
    order = block_order[0]
    factor = jnp.repeat(jnp.exp2(scale_exps[0].astype(jnp.float32)), CBLK, axis=0)
    keys_ctx = (cache_keys[0].astype(jnp.float32) * factor[:, :, 0:1]).astype(jnp.bfloat16)
    vals_ctx = (cache_values[0].astype(jnp.float32) * factor[:, :, 1:2]).astype(jnp.bfloat16)
    own_keys = jnp.concatenate([keys_ctx, span_keys[0]], axis=0)
    own_vals = jnp.concatenate([vals_ctx, span_values[0]], axis=0)
    own_block = jnp.stack([own_keys, own_vals], axis=2)
    index = jnp.arange(tok_local, dtype=jnp.int32)
    pos_query = table_lookup(order, 2 * mine + index // half) * half + index % half
    group_size = head_local // kv_local
    initial = (
        jnp.full((kv_local, group_size, tok_local), -jnp.inf, jnp.float32),
        jnp.zeros((kv_local, group_size, tok_local), jnp.float32),
        jnp.zeros((kv_local, group_size, tok_local, width), jnp.float32),
    )
    carry = attend(
        initial,
        lax.all_gather(own_block, "ctx", axis=0, tiled=True),
        grouped,
        pos_query,
        order,
        half,
        cache_len,
        rows_dev,
    )
    best, total, accum = carry
    mixed = accum / total[..., None]
    rotated = jnp.dot(mixed.reshape(-1, width), hadamard(width))
    rotated = rotated.reshape(kv_local, group_size, tok_local, width).transpose(2, 0, 1, 3)
    result = rotated.reshape(1, tok_local, head_local, width).astype(jnp.bfloat16)
    return shifted(result, "pipe", 1)


def solution(mesh):
    placed = (
        P("pipe", "ctx", "tp", None),
        P("pipe", "ctx", "tp", None),
        P("pipe", "ctx", "tp", None),
        P("pipe", "ctx", "tp", None),
        P("pipe", "ctx", "tp", None),
        P("pipe", "ctx", "tp", None),
        P("pipe", None),
    )
    return jax.shard_map(
        on_device,
        mesh=mesh,
        in_specs=placed,
        out_specs=P("pipe", "ctx", "tp", None),
        check_vma=False,
    )
```

profile of v0, /device:TPU:1, one launch (start us, length us, event | category | flops | bytes accessed | tf_op | source)
XLA Modules:
  0.0 190.2 jit_solution(14502393834735405781)
XLA Ops:
  6.5 0.0 copy-start
  6.5 0.0 all-gather.2.cloned.1.call-start
  6.5 0.8 exponential_bitcast_fusion
  7.3 0.1 copy.16
  7.4 0.1 broadcast_in_dim.66
  7.5 0.1 reshape.263
  7.6 0.9 copy.34
  8.4 0.9 copy.33
  9.3 0.9 fusion.29
  10.2 0.7 pad_maximum_fusion
  10.9 0.0 all-gather.2.cloned.1.call-update
  11.0 0.8 select_reduce_fusion.1
  11.9 0.9 select_reduce_fusion
  12.8 0.2 compare_or_fusion
  13.0 78.2 %all-gather.2.cloned.1.call-done = bf16[3072,4,2,128]{3,0,1,2:T(8,128)(2,1)} async-done(((bf16[96,4,2,128]{3,0,1,2:T(8,128)(2,1)}), bf16[3072,4,2,128]{3,0,1,2:T(8,128)(2,1)}) %all-gather.2.cloned.1.call-update) | async-done | bytes 6291472 | tf_op jit(solution)/shard_map/all_gather | solution.py:82
  91.2 0.0 copy-done
  91.2 20.1 %fusion.2 = (f32[4,16,64]{2,1,0:T(8,128)S(1)}, f32[4,3072,64,16]{1,2,3,0:T(8,128)}) fusion(pred[64,3072]{1,0:T(8,128)(4,1)S(1)} %compare_or_fusion, bf16[64,4,16,128]{3,2,1,0:T(8,128)(2,1)S(1)} %bitcast.69, bf16[3072,4,2,128]{3,0,1,2:T(8,128)(2,1)} %all-gather.2.cloned.1.call-done), kind=kOutput, calls=%fused_computation.4 | convolution fusion | flops 3258970112 | bytes 54738944 | tf_op jit(solution)/shard_map/tgqd,kgd->gqtk/dot_general | solution.py:42
  111.4 21.7 %fusion = f32[4,16,64]{2,1,0:T(8,128)S(1)} fusion(f32[4,3072,64,16]{1,2,3,0:T(8,128)} %get-tuple-element.10, f32[4,16,64]{2,1,0:T(8,128)S(1)} %compare_select_fusion, pred[64,3072]{1,0:T(8,128)(4,1)S(1)} %compare_or_fusion), kind=kLoop, calls=%fused_computation.2 | loop fusion | flops 50327552 | bytes 50561024 | tf_op jit(solution)/shard_map/reduce_sum | solution.py:48
  133.1 19.8 %fusion.14 = bf16[4,16,64,128]{3,2,1,0:T(8,128)(2,1)S(1)} fusion(bf16[3072,4,2,128]{3,0,1,2:T(8,128)(2,1)} %all-gather.2.cloned.1.call-done, f32[4,3072,64,16]{1,2,3,0:T(8,128)} %get-tuple-element.10, f32[4,16,64]{2,1,0:T(8,128)S(1)} %compare_select_fusion, pred[64,3072]{1,0:T(8,128)(4,1)S(1)} %compare_or_fusion, f32[4,16,64]{2,1,0:T(8,128)S(1)} %get-tuple-element.6, ...), kind=kOutput, calls=%fused_computation.13 | convolution fusion | flops 3407806464 | bytes 54828032 | tf_op jit(solution)/shard_map/dot_general | solution.py:92
  152.9 0.7 copy.21
  153.5 3.3 %collective-permute-start = (bf16[1,64,64,128]{3,2,1,0:T(8,128)(2,1)S(1)}, bf16[1,64,64,128]{3,2,1,0:T(8,128)(2,1)S(1)}, u32[]{:S(2)}, u32[]{:S(2)}) collective-permute-start(bf16[1,64,64,128]{3,2,1,0:T(8,128)(2,1)S(1)} %copy.21), channel_id=1, source_target_pairs={{0,64},{64,128},{128,192},{192,256},{256,320},{320,384},{384,448},... | collective-permute-start | bytes 3145736 | tf_op jit(solution)/shard_map/ppermute | solution.py:12
  156.8 25.6 %collective-permute-done = bf16[1,64,64,128]{3,2,1,0:T(8,128)(2,1)S(1)} collective-permute-done((bf16[1,64,64,128]{3,2,1,0:T(8,128)(2,1)S(1)}, bf16[1,64,64,128]{3,2,1,0:T(8,128)(2,1)S(1)}, u32[]{:S(2)}, u32[]{:S(2)}) %collective-permute-start) | collective-permute-done | bytes 1048608 | tf_op jit(solution)/shard_map/ppermute | solution.py:12
  182.4 1.0 copy.36
  (14 shorter events, 0.1 us)
Async XLA Ops:
  6.5 84.7 %copy-start = (bf16[1,64,64,128]{3,2,1,0:T(8,128)(2,1)S(1)}, bf16[1,64,64,128]{3,2,1,0:T(8,128)(2,1)}, u32[]{:S(2)}) copy-start(bf16[1,64,64,128]{3,2,1,0:T(8,128)(2,1)} %param.7) | copy-start | bytes 3145732
  6.5 84.7 %all-gather.2.cloned.1.call-start = ((), (), s32[]{:S(2)}) async-start(), calls=%async_computation | async-start | bytes 6488064 | tf_op jit(solution)/shard_map/all_gather | solution.py:82
  153.5 28.8 %collective-permute-start = (bf16[1,64,64,128]{3,2,1,0:T(8,128)(2,1)S(1)}, bf16[1,64,64,128]{3,2,1,0:T(8,128)(2,1)S(1)}, u32[]{:S(2)}, u32[]{:S(2)}) collective-permute-start(bf16[1,64,64,128]{3,2,1,0:T(8,128)(2,1)S(1)} %copy.21), channel_id=1, source_target_pairs={{0,64},{64,128},{128,192},{192,256},{256,320},{320,384},{384,448},... | collective-permute-start | bytes 3145736 | tf_op jit(solution)/shard_map/ppermute | solution.py:12
Sparse Core Ops, SparseCore 0:
  11.1 80.1 all-gather.1
where the time goes:
time: 191 us; the launch traced here: 190 us
  waiting for transfers between devices  104 us (54%)
  matrix products  39.9 us (21%)
  other arithmetic  26 us (14%)
  between operations  13.5 us (7%)
  local copies, waits for them, and re-layouts  3.63 us (2%)
  starting transfers between devices  3.28 us (2%)
    all_gather x1, waiting for transfers between devices, on_device(): lax.all_gather(own_block, 'ctx', axis=0, tiled=True)  78.2 us
    ppermute x1, waiting for transfers between devices, shifted(): return lax.ppermute(value, axis, pairs)  25.6 us
    reduce_sum x1, other arithmetic, attend(): total = total * rescale + jnp.sum(expo, axis=-1)  21.7 us
    dot_general x1, matrix products, attend(): jnp.einsum('tgqd,kgd->gqtk', grouped, keys, preferred_element_type=jnp.fl...  20.1 us
    dot_general x1, matrix products, on_device(): rotated = jnp.dot(mixed.reshape(-1, width), hadamard(width))  19.8 us
  transfers between devices with their start and end apart: 2, of which 2 were waited for; matrix products, arithmetic and copies ran while one was open for 1% of the time, Pallas kernels for 0%

commit v1 on v0

--- a/solution.py
+++ b/solution.py
@@ -4,6 +4,11 @@
 from jax.sharding import PartitionSpec as P
 
 CBLK = 16
+
+
+def gather_over(array, axis, dim):
+    repeated = jnp.stack([array] * lax.axis_size(axis))
+    return jnp.concatenate(lax.all_to_all(repeated, axis, 0, 0), axis=dim)
 
 
 def shifted(value, axis, steps):
@@ -79,7 +84,7 @@
     )
     carry = attend(
         initial,
-        lax.all_gather(own_block, "ctx", axis=0, tiled=True),
+        gather_over(own_block, "ctx", 0),
         grouped,
         pos_query,
         order,

time: 191 us -> 263 us (1.38)
  waiting for transfers between devices: 104 us -> 166 us
  between operations: 13.5 us -> 0.16 us
  starting transfers between devices: 3.28 us -> 15 us
  local copies, waits for them, and re-layouts: 3.63 us -> 13 us
    all_to_all x0 -> x1, waiting for transfers between devices: none -> 139 us  [gather_over(): return jnp.concatenate(lax.all_to_all(repeated, axis, 0, 0), axis=dim)]
    all_gather x1 -> x0, waiting for transfers between devices: 78.2 us -> none  [on_device(): lax.all_gather(own_block, 'ctx', axis=0, tiled=True)]
    all_to_all x0 -> x1, starting transfers between devices: none -> 11.3 us  [gather_over(): return jnp.concatenate(lax.all_to_all(repeated, axis, 0, 0), axis=dim)]
    all_to_all x0 -> x1, local copies, waits for them, and re-layouts: none -> 6.68 us  [gather_over(): return jnp.concatenate(lax.all_to_all(repeated, axis, 0, 0), axis=dim)]
    another operation x0 -> x2, local copies, waits for them, and re-layouts: none -> 4.22 us  [the longest x1 4.19 us: gather_over(): repeated = jnp.stack([array] * lax.axis_size(axis))]
where the time goes in v1:
time: 263 us; the launch traced here: 261 us
  waiting for transfers between devices  166 us (63%)
  matrix products  39.9 us (15%)
  other arithmetic  27.4 us (10%)
  starting transfers between devices  15 us (6%)
  local copies, waits for them, and re-layouts  13 us (5%)
    all_to_all x1, waiting for transfers between devices, gather_over(): return jnp.concatenate(lax.all_to_all(repeated, axis, 0, 0), axis=dim)  139 us
    ppermute x1, waiting for transfers between devices, shifted(): return lax.ppermute(value, axis, pairs)  26.9 us
    reduce_sum x1, other arithmetic, attend(): total = total * rescale + jnp.sum(expo, axis=-1)  21.7 us
    dot_general x1, matrix products, attend(): jnp.einsum('tgqd,kgd->gqtk', grouped, keys, preferred_element_type=jnp.fl...  20.2 us
    dot_general x1, matrix products, on_device(): rotated = jnp.dot(mixed.reshape(-1, width), hadamard(width))  19.8 us
    all_to_all x1, starting transfers between devices, gather_over(): return jnp.concatenate(lax.all_to_all(repeated, axis, 0, 0), axis=dim)  11.3 us
    all_to_all x1, local copies, waits for them, and re-layouts, gather_over(): return jnp.concatenate(lax.all_to_all(repeated, axis, 0, 0), axis=dim)  6.68 us
  transfers between devices with their start and end apart: 2, of which 2 were waited for; matrix products, arithmetic and copies ran while one was open for 1% of the time, Pallas kernels for 0%

profile of v1, /device:TPU:1, one launch (start us, length us, event | category | flops | bytes accessed | tf_op | source)
XLA Modules:
  0.0 261.3 jit_solution(14891874289135089742)
XLA Ops:
  0.0 0.0 copy-start
  0.0 0.8 exponential_bitcast_fusion
  0.8 0.1 copy.21
  0.9 0.1 broadcast_in_dim.66
  1.0 0.1 reshape.268
  1.1 0.1 copy.22
  1.1 0.1 copy.23
  1.2 0.9 fusion.30
  2.1 0.9 fusion.29
  3.0 1.0 maximum_bitcast_fusion
  4.0 0.1 pad_maximum_fusion
  4.2 4.2 %stack.11 = bf16[32,96,4,2,128]{4,1,2,3,0:T(8,128)(2,1)} broadcast(bf16[96,4,2,128]{3,0,1,2:T(8,128)(2,1)S(1)} %copy.24), dimensions={1,2,3,4} | broadcast | bytes 6488064 | tf_op jit(solution)/shard_map/stack | solution.py:10
  8.3 11.3 %all-to-all-start = ((bf16[32,96,4,2,128]{4,1,2,3,0:T(8,128)(2,1)}), bf16[32,96,4,2,128]{4,1,2,3,0:T(8,128)(2,1)}, u32[]{:S(2)}, u32[]{:S(2)}) async-start(bf16[32,96,4,2,128]{4,1,2,3,0:T(8,128)(2,1)} %stack.11), calls=%async_computation | async-start | bytes 12582912 | tf_op jit(solution)/shard_map/all_to_all | solution.py:11
  19.8 0.8 select_reduce_fusion.1
  20.6 0.9 select_reduce_fusion
  21.5 0.2 compare_or_fusion
  21.7 138.9 %all-to-all-done = bf16[32,96,4,2,128]{4,1,2,3,0:T(8,128)(2,1)} async-done(((bf16[32,96,4,2,128]{4,1,2,3,0:T(8,128)(2,1)}), bf16[32,96,4,2,128]{4,1,2,3,0:T(8,128)(2,1)}, u32[]{:S(2)}, u32[]{:S(2)}) %all-to-all-start) | async-done | bytes 6291488 | tf_op jit(solution)/shard_map/all_to_all | solution.py:11
  160.6 6.7 %copy.25 = bf16[32,96,4,2,128]{4,1,0,2,3:T(8,128)(2,1)} copy(bf16[32,96,4,2,128]{4,1,2,3,0:T(8,128)(2,1)} %all-to-all-done) | data formatting | bytes 12582912 | tf_op jit(solution)/shard_map/all_to_all | solution.py:11
  167.3 0.0 copy-done
  167.3 20.2 %fusion.2 = (f32[4,16,64]{2,1,0:T(8,128)S(1)}, f32[4,3072,64,16]{1,2,3,0:T(8,128)}) fusion(pred[64,3072]{1,0:T(8,128)(4,1)S(1)} %compare_or_fusion, bf16[64,4,16,128]{3,2,1,0:T(8,128)(2,1)S(1)} %bitcast.66, bf16[3072,4,2,128]{3,0,1,2:T(8,128)(2,1)} %bitcast.67), kind=kOutput, calls=%fused_computation.4 | convolution fusion | flops 3258970112 | bytes 54738944 | tf_op jit(solution)/shard_map/tgqd,kgd->gqtk/dot_general | solution.py:47
  187.5 0.0 copy-start.1
  187.5 21.7 %fusion = f32[4,16,64]{2,1,0:T(8,128)S(1)} fusion(f32[4,3072,64,16]{1,2,3,0:T(8,128)} %get-tuple-element.10, f32[4,16,64]{2,1,0:T(8,128)S(1)} %compare_select_fusion, pred[64,3072]{1,0:T(8,128)(4,1)S(1)} %compare_or_fusion), kind=kLoop, calls=%fused_computation.2 | loop fusion | flops 50327552 | bytes 50561024 | tf_op jit(solution)/shard_map/reduce_sum | solution.py:53
  209.3 19.8 %fusion.14 = bf16[4,16,64,128]{3,2,1,0:T(8,128)(2,1)S(1)} fusion(bf16[3072,4,2,128]{3,0,1,2:T(8,128)(2,1)} %bitcast.68, f32[4,3072,64,16]{1,2,3,0:T(8,128)} %get-tuple-element.10, f32[4,16,64]{2,1,0:T(8,128)S(1)} %compare_select_fusion, pred[64,3072]{1,0:T(8,128)(4,1)S(1)} %compare_or_fusion, f32[4,16,64]{2,1,0:T(8,128)S(1)} %get-tuple-element.6, ...), kind=kOutput, calls=%fused_computation.13 | convolution fusion | flops 3407806464 | bytes 54828032 | tf_op jit(solution)/shard_map/dot_general | solution.py:97
  229.1 0.7 copy.27
  229.7 3.6 %collective-permute-start = (bf16[1,64,64,128]{3,2,1,0:T(8,128)(2,1)S(1)}, bf16[1,64,64,128]{3,2,1,0:T(8,128)(2,1)S(1)}, u32[]{:S(2)}, u32[]{:S(2)}) collective-permute-start(bf16[1,64,64,128]{3,2,1,0:T(8,128)(2,1)S(1)} %copy.27), channel_id=1, source_target_pairs={{0,64},{64,128},{128,192},{192,256},{256,320},{320,384},{384,448},... | collective-permute-start | bytes 3145736 | tf_op jit(solution)/shard_map/ppermute | solution.py:17
  233.4 26.9 %collective-permute-done = bf16[1,64,64,128]{3,2,1,0:T(8,128)(2,1)S(1)} collective-permute-done((bf16[1,64,64,128]{3,2,1,0:T(8,128)(2,1)S(1)}, bf16[1,64,64,128]{3,2,1,0:T(8,128)(2,1)S(1)}, u32[]{:S(2)}, u32[]{:S(2)}) %collective-permute-start) | collective-permute-done | bytes 1048608 | tf_op jit(solution)/shard_map/ppermute | solution.py:17
  260.3 1.0 copy.36
  261.3 0.0 copy-done.1
  (13 shorter events, 0.1 us)
Async XLA Ops:
  0.0 167.3 %copy-start = (bf16[1,64,64,128]{3,2,1,0:T(8,128)(2,1)S(1)}, bf16[1,64,64,128]{3,2,1,0:T(8,128)(2,1)}, u32[]{:S(2)}) copy-start(bf16[1,64,64,128]{3,2,1,0:T(8,128)(2,1)} %param.7) | copy-start | bytes 3145732
  8.3 152.3 %all-to-all-start = ((bf16[32,96,4,2,128]{4,1,2,3,0:T(8,128)(2,1)}), bf16[32,96,4,2,128]{4,1,2,3,0:T(8,128)(2,1)}, u32[]{:S(2)}, u32[]{:S(2)}) async-start(bf16[32,96,4,2,128]{4,1,2,3,0:T(8,128)(2,1)} %stack.11), calls=%async_computation | async-start | bytes 12582912 | tf_op jit(solution)/shard_map/all_to_all | solution.py:11
  187.5 73.8 %copy-start.1 = (bf16[1,64,64,128]{3,2,1,0:T(8,128)(2,1)S(1)}, bf16[1,64,64,128]{3,2,1,0:T(8,128)(2,1)}, u32[]{:S(2)}) copy-start(bf16[1,64,64,128]{3,2,1,0:T(8,128)(2,1)} %param.7) | copy-start | bytes 3145732
  229.7 30.6 %collective-permute-start = (bf16[1,64,64,128]{3,2,1,0:T(8,128)(2,1)S(1)}, bf16[1,64,64,128]{3,2,1,0:T(8,128)(2,1)S(1)}, u32[]{:S(2)}, u32[]{:S(2)}) collective-permute-start(bf16[1,64,64,128]{3,2,1,0:T(8,128)(2,1)S(1)} %copy.27), channel_id=1, source_target_pairs={{0,64},{64,128},{128,192},{192,256},{256,320},{320,384},{384,448},... | collective-permute-start | bytes 3145736 | tf_op jit(solution)/shard_map/ppermute | solution.py:17
